TPU v7x, 32 devices: a whole 2x2x4 slice. The times are simulated.
32 devices in a mesh: row: 8 (over z, y), col: 4 (over x, core).
Axes of the slice: x: 2, y: 2, z: 4, core: 2. Of those that a mesh axis runs over, the one named last changes fastest.
Arguments:
- inv_blocks: bfloat16 [2048, 2048], P('row', 'col'), may hold values from -0.125 to 0.125
- factor: bfloat16 [4, 2048, 128], P('col', 'row'), may hold values from -2.3125 to 2.3125
- pattern: int32 [4, 16], P('col', 'row'), may hold values from 0 to 1, as said below
- diag_inv: float32 [4, 128, 128], P(None, 'row', 'col'), may hold values from -12 to 12
Outputs:
- inverse_panel: bfloat16 [4, 128, 2048], P(None, 'col', 'row')
- diag_block: float32 [4, 128, 128], P(None, 'row', 'col')
Inputs may be any that keep to these rules, and one draw needn't show every extreme that they name: pattern is 0 or 1; each supernode has its own share of 1s.
All inputs are finite; a program needn't handle non-finite values.
Results may differ from a plain program's by a relative error of at most 0.0005.
Values may be sent and summed in bfloat16 or wider, within the bound.
No kernel may reach another device: no remote copies, remote signals or barrier semaphores. Data moves between devices by JAX's collectives and lax.ppermute only.
A program may use at most 64 MiB of HBM per device.

v0:
```python
import jax
import jax.numpy as jnp
from jax import lax
from jax.sharding import PartitionSpec as P


def broadcast(block, axis, owner):
    block = jnp.where(lax.axis_index(axis) == owner, block, jnp.zeros_like(block))
    return lax.psum(block, axis)


def on_device(inv_blocks, factor, pattern, diag_inv):
    width = factor.shape[2]
    n_row = lax.axis_size("row")
    n_col = lax.axis_size("col")
    ratio = n_row // n_col
    col_place = lax.axis_index("col")
    row_place = lax.axis_index("row")
    keep = jnp.repeat(pattern, width, axis=1).astype(jnp.bfloat16)
    own_masked = factor * keep[:, :, None]
    level_rows = lax.all_gather(own_masked, "col", axis=0, tiled=True)
    pieces = []
    for offset in range(ratio):
        pieces.append(broadcast(level_rows, "row", col_place * ratio + offset))
    column_rows = jnp.concatenate(pieces, axis=1)
    level_float = level_rows.astype(jnp.float32)
    row_span = width // n_row
    share = lax.psum_scatter(
        -jnp.einsum("ij,sjw->wsi", inv_blocks, column_rows, preferred_element_type=jnp.float32),
        "col",
        scatter_dimension=0,
        tiled=True,
    )
    inner = jnp.einsum("siw,vsi->swv", level_float, share, precision=lax.Precision.HIGHEST)
    inner_total = lax.psum(inner, "row")
    inner_sum = lax.dynamic_slice_in_dim(inner_total, row_place * row_span, row_span, 1)
    inverse_panel = jnp.transpose(share, (1, 0, 2)).astype(jnp.bfloat16)
    return (inverse_panel, diag_inv - inner_sum)


def solution(mesh):
    return jax.shard_map(
        on_device,
        mesh=mesh,
        in_specs=(P("row", "col"), P("col", "row", None), P("col", "row"), P(None, "row", "col")),
        out_specs=(P(None, "col", "row"), P(None, "row", "col")),
        check_vma=False,
    )
```

profile of v0, /device:TPU:0, one launch (start us, length us, event | category | flops | bytes accessed | tf_op | source)
XLA Modules:
  0.0 197.1 jit_solution(16191956537070518140)
XLA Ops:
  7.2 0.0 copy-start
  7.2 0.0 all-reduce.6.cloned.1.call-start
  7.2 0.0 copy-start.3
  7.2 0.7 copy-done.3
  7.9 0.1 broadcast_bitcast_fusion
  8.0 0.9 broadcast_multiply_fusion
  8.9 7.2 %all_gather.3 = bf16[4,256,128]{2,1,0:T(8,128)(2,1)S(1)} all-gather(bf16[1,256,128]{2,1,0:T(8,128)(2,1)S(1)} %broadcast_multiply_fusion), channel_id=1, replica_groups=mesh['row'=8,'col'=4] {'col'}, dimensions={0}, use_global_device_ids=true | all-gather | bytes 327680 | tf_op jit(solution)/shard_map/all_gather | solution.py:21
  16.2 0.1 copy.7
  16.3 0.8 broadcast_select_fusion.1
  17.2 0.0 all-reduce.6.cloned.1.call-update
  17.2 0.0 reduce-scatter.2.cloned.1.call-start
  17.2 74.1 %all-reduce.6.cloned.1.call-done = (bf16[4,256,128]{1,2,0:T(8,128)(2,1)}, bf16[4,256,128]{1,2,0:T(8,128)(2,1)}) async-done(((bf16[4,256,128]{1,2,0:T(8,128)(2,1)}, bf16[4,256,128]{1,2,0:T(8,128)(2,1)}), (bf16[4,256,128]{1,2,0:T(8,128)(2,1)}, bf16[4,256,128]{1,2,0:T(8,128)(2,1)})) %all-reduce.6.cloned.1.call-update) | async-done | bytes 524304 | tf_op jit(solution)/shard_map/psum | solution.py:9
  91.4 0.0 copy-done
  91.4 2.1 %fusion = f32[128,4,256]{2,0,1:T(8,128)} fusion(bf16[4,256,128]{1,2,0:T(8,128)(2,1)} %get-tuple-element.2, bf16[4,256,128]{1,2,0:T(8,128)(2,1)} %get-tuple-element.3, bf16[256,512]{1,0:T(8,128)(2,1)S(1)} %copy-done), kind=kOutput, calls=%fused_computation.1 | convolution fusion | flops 135397376 | bytes 1310720 | tf_op jit(solution)/shard_map/ij,sjw->wsi/dot_general | solution.py:29
  93.5 0.0 reduce-scatter.2.cloned.1.call-update
  93.5 0.0 all-reduce.4.cloned.1.call-start
  93.6 21.1 %reduce-scatter.2.cloned.1.call-done = f32[32,4,256]{2,0,1:T(8,128)} async-done(((f32[128,4,256]{2,0,1:T(8,128)}), f32[32,4,256]{2,0,1:T(8,128)}) %reduce-scatter.2.cloned.1.call-update) | async-done | bytes 131088 | tf_op jit(solution)/shard_map/reduce_scatter | solution.py:28
  114.7 2.0 %fusion.6 = f32[4,128,32]{2,1,0:T(8,128)} fusion(bf16[4,256,128]{2,1,0:T(8,128)(2,1)S(1)} %all_gather.3, f32[32,4,256]{2,0,1:T(8,128)} %reduce-scatter.2.cloned.1.call-done), kind=kOutput, calls=%fused_computation.14 | convolution fusion | flops 50331648 | bytes 458752 | tf_op jit(solution)/shard_map/siw,vsi->swv/dot_general | solution.py:34
  116.7 0.0 copy-start.1
  116.7 0.0 all-reduce.4.cloned.1.call-update
  116.8 0.9 copy-done.1
  117.6 0.0 copy-start.2
  117.7 0.6 convert_bitcast_fusion
  118.3 70.9 %all-reduce.4.cloned.1.call-done = f32[4,128,32]{2,1,0:T(8,128)} async-done(((f32[4,128,32]{2,1,0:T(8,128)}), f32[4,128,32]{2,1,0:T(8,128)}) %all-reduce.4.cloned.1.call-update) | async-done | bytes 65552 | tf_op jit(solution)/shard_map/psum | solution.py:35
  189.2 0.0 copy-done.2
  189.2 1.4 dynamic-slice_subtract_fusion
  (1 shorter events, 0.0 us)
Async XLA Ops:
  7.2 84.2 %copy-start = (bf16[256,512]{1,0:T(8,128)(2,1)S(1)}, bf16[256,512]{1,0:T(8,128)(2,1)}, u32[]{:S(2)}) copy-start(bf16[256,512]{1,0:T(8,128)(2,1)} %param.4) | copy-start | bytes 786436
  7.2 84.2 %all-reduce.6.cloned.1.call-start = ((), (), s32[]{:S(2)}) async-start(), calls=%async_computation.3 | async-start | bytes 1048576 | tf_op jit(solution)/shard_map/psum | solution.py:9
  7.2 0.7 copy-start.3
  17.2 97.6 %reduce-scatter.2.cloned.1.call-start = ((), (), s32[]{:S(2)}) async-start(), calls=%async_computation.1 | async-start | bytes 655360 | tf_op jit(solution)/shard_map/reduce_scatter | solution.py:28
  93.5 95.6 %all-reduce.4.cloned.1.call-start = ((), (), s32[]{:S(2)}) async-start(), calls=%async_computation.2 | async-start | bytes 524288 | tf_op jit(solution)/shard_map/psum | solution.py:35
  116.7 0.9 copy-start.1
  117.6 71.5 %copy-start.2 = (f32[4,16,32]{2,1,0:T(8,128)S(1)}, f32[4,16,32]{2,1,0:T(8,128)}, u32[]{:S(2)}) copy-start(f32[4,16,32]{2,1,0:T(8,128)} %param.7) | copy-start | bytes 24580
Sparse Core Ops, SparseCore 0:
  17.3 74.0 all-reduce.5
  93.9 20.8 reduce-scatter.1
  118.1 71.0 all-reduce.3
where the time goes:
time: 197 us
  waiting for transfers between devices  166 us (84%)
  between operations  13.8 us (7%)
  blocking collectives  7.22 us (4%)
  matrix products  4.16 us (2%)
  other arithmetic  3.79 us (2%)
    psum x1, waiting for transfers between devices, broadcast(): return lax.psum(block, axis)  74.1 us
    psum x1, waiting for transfers between devices, on_device(): inner_total = lax.psum(inner, 'row')  70.9 us
    reduce_scatter x1, waiting for transfers between devices, on_device(): lax.psum_scatter(-jnp.einsum('ij,sjw->wsi', inv_blocks, column_rows, pref...  21.1 us
    all_gather x1, blocking collectives, on_device(): level_rows = lax.all_gather(own_masked, 'col', axis=0, tiled=True)  7.22 us
  transfers between devices with their start and end apart: 3, of which 3 were waited for; matrix products, arithmetic and copies ran while one was open for 0% of the time, Pallas kernels for 0%

commit v1 on v0

--- a/solution.py
+++ b/solution.py
@@ -6,7 +6,7 @@
 
 def broadcast(block, axis, owner):
     block = jnp.where(lax.axis_index(axis) == owner, block, jnp.zeros_like(block))
-    return lax.psum(block, axis)
+    return jnp.sum(lax.all_gather(block, axis), axis=0)
 
 
 def on_device(inv_blocks, factor, pattern, diag_inv):

time: 197 us -> 223 us (1.13)
  waiting for transfers between devices: 166 us -> 189 us
  other arithmetic: 3.79 us -> 9.23 us
    all_gather x0 -> x2, waiting for transfers between devices: none -> 97.4 us  [broadcast(): return jnp.sum(lax.all_gather(block, axis), axis=0)]
    psum x1 -> x0, waiting for transfers between devices: 74.1 us -> none  [broadcast(): return lax.psum(block, axis)]
    reduce_sum x0 -> x2, other arithmetic: none -> 3.85 us  [broadcast(): return jnp.sum(lax.all_gather(block, axis), axis=0)]
  transfers between devices with their start and end apart: 3 -> 4, of which waited for: 3 -> 4; matrix products, arithmetic and copies ran while one was open for 0% -> 2% of each run, Pallas kernels for 0% -> 0%
where the time goes in v1:
time: 223 us
  waiting for transfers between devices  189 us (85%)
  between operations  13.8 us (6%)
  other arithmetic  9.23 us (4%)
  blocking collectives  7.22 us (3%)
  matrix products  3.14 us (1%)
    all_gather x2, waiting for transfers between devices, broadcast(): return jnp.sum(lax.all_gather(block, axis), axis=0)  97.4 us
    psum x1, waiting for transfers between devices, on_device(): inner_total = lax.psum(inner, 'row')  70.7 us
    reduce_scatter x1, waiting for transfers between devices, on_device(): lax.psum_scatter(-jnp.einsum('ij,sjw->wsi', inv_blocks, column_rows, pref...  20.3 us
    all_gather x1, blocking collectives, on_device(): level_rows = lax.all_gather(own_masked, 'col', axis=0, tiled=True)  7.22 us
  transfers between devices with their start and end apart: 4, of which 4 were waited for; matrix products, arithmetic and copies ran while one was open for 2% of the time, Pallas kernels for 0%

profile of v1, /device:TPU:0, one launch (start us, length us, event | category | flops | bytes accessed | tf_op | source)
XLA Modules:
  0.0 223.1 jit_solution(18065638594800699683)
XLA Ops:
  7.2 0.0 copy-start
  7.2 0.0 all-gather.5.cloned.1.call-start
  7.2 0.7 convert_bitcast_fusion.1
  7.9 0.1 broadcast_bitcast_fusion
  8.0 0.9 broadcast_multiply_fusion
  8.9 7.2 %all_gather.15 = bf16[4,256,128]{2,1,0:T(8,128)(2,1)S(1)} all-gather(bf16[1,256,128]{2,1,0:T(8,128)(2,1)S(1)} %broadcast_multiply_fusion), channel_id=1, replica_groups=mesh['row'=8,'col'=4] {'col'}, dimensions={0}, use_global_device_ids=true | all-gather | bytes 327680 | tf_op jit(solution)/shard_map/all_gather | solution.py:21
  16.2 0.8 broadcast_select_fusion.1
  17.0 0.0 all-gather.5.cloned.1.call-update
  17.0 0.0 all-gather.7.cloned.1.call-start
  17.1 0.7 all-gather.7.cloned.1.call-update
  17.8 0.0 reduce-scatter.2.cloned.1.call-start
  17.8 49.7 %all-gather.5.cloned.1.call-done = bf16[32,256,128]{2,1,0:T(8,128)(2,1)} async-done(((bf16[4,256,128]{2,1,0:T(8,128)(2,1)}), bf16[32,256,128]{2,1,0:T(8,128)(2,1)}) %all-gather.5.cloned.1.call-update) | async-done | bytes 2097168 | tf_op jit(solution)/shard_map/all_gather | solution.py:9
  67.6 1.9 reduce_sum.24
  69.5 0.1 copy.8
  69.6 47.7 %all-gather.7.cloned.1.call-done = bf16[32,256,128]{2,1,0:T(8,128)(2,1)} async-done(((bf16[4,256,128]{2,1,0:T(8,128)(2,1)}), bf16[32,256,128]{2,1,0:T(8,128)(2,1)}) %all-gather.7.cloned.1.call-update) | async-done | bytes 2097168 | tf_op jit(solution)/shard_map/all_gather | solution.py:9
  117.3 1.9 reduce_sum.25
  119.3 0.0 copy-start.1
  119.3 0.1 copy.9
  119.4 0.0 copy-done
  119.4 1.1 fusion
  120.6 0.0 reduce-scatter.2.cloned.1.call-update
  120.6 0.0 all-reduce.2.cloned.1.call-start
  120.6 20.3 %reduce-scatter.2.cloned.1.call-done = f32[32,4,256]{2,0,1:T(8,128)} async-done(((f32[128,4,256]{2,0,1:T(8,128)}), f32[32,4,256]{2,0,1:T(8,128)}) %reduce-scatter.2.cloned.1.call-update) | async-done | bytes 131088 | tf_op jit(solution)/shard_map/reduce_scatter | solution.py:28
  140.9 2.0 fusion.6
  142.9 0.0 all-reduce.2.cloned.1.call-update
  143.0 1.5 convert_bitcast_fusion
  144.5 70.7 %all-reduce.2.cloned.1.call-done = f32[4,128,32]{2,1,0:T(8,128)} async-done(((f32[4,128,32]{2,1,0:T(8,128)}), f32[4,128,32]{2,1,0:T(8,128)}) %all-reduce.2.cloned.1.call-update) | async-done | bytes 65552 | tf_op jit(solution)/shard_map/psum | solution.py:35
  215.2 0.0 copy-done.1
  215.2 1.4 dynamic-slice_subtract_fusion
Async XLA Ops:
  7.2 112.3 %copy-start = (bf16[256,512]{1,0:T(8,128)(2,1)S(1)}, bf16[256,512]{1,0:T(8,128)(2,1)}, u32[]{:S(2)}) copy-start(bf16[256,512]{1,0:T(8,128)(2,1)} %param.4) | copy-start | bytes 786436
  7.2 60.4 %all-gather.5.cloned.1.call-start = ((), (), s32[]{:S(2)}) async-start(), calls=%async_computation.3 | async-start | bytes 2359296 | tf_op jit(solution)/shard_map/all_gather | solution.py:9
  17.0 100.3 %all-gather.7.cloned.1.call-start = ((), (), s32[]{:S(2)}) async-start(), calls=%async_computation.4 | async-start | bytes 2359296 | tf_op jit(solution)/shard_map/all_gather | solution.py:9
  17.8 123.1 %reduce-scatter.2.cloned.1.call-start = ((), (), s32[]{:S(2)}) async-start(), calls=%async_computation.1 | async-start | bytes 655360 | tf_op jit(solution)/shard_map/reduce_scatter | solution.py:28
  119.3 95.9 %copy-start.1 = (f32[4,16,32]{2,1,0:T(8,128)S(1)}, f32[4,16,32]{2,1,0:T(8,128)}, u32[]{:S(2)}) copy-start(f32[4,16,32]{2,1,0:T(8,128)} %param.7) | copy-start | bytes 24580
  120.6 94.6 %all-reduce.2.cloned.1.call-start = ((), (), s32[]{:S(2)}) async-start(), calls=%async_computation.2 | async-start | bytes 524288 | tf_op jit(solution)/shard_map/psum | solution.py:35
Sparse Core Ops, SparseCore 0:
  17.2 50.3 all-gather.4
  69.7 47.6 all-gather.6
  120.7 20.1 reduce-scatter.1
  144.1 71.0 all-reduce.1
